TPU v7x, 32 devices: a whole 2x2x4 slice. The times are simulated.
32 devices in a mesh: groups: 2 (over x), seq: 16 (over z, y, core).
Axes of the slice: x: 2, y: 2, z: 4, core: 2. Of those that a mesh axis runs over, the one named last changes fastest.
Arguments:
- hidden: bfloat16 [4096, 8192], P(('groups', 'seq')), parts along dimension 0, may hold values from -6 to 6
- q_base: bfloat16 [4096, 8192], P(('groups', 'seq')), parts along dimension 0, may hold values from -8 to 8
- base_key_weight: bfloat16 [4096, 1024], P(('groups', 'seq')), parts along dimension 0, may hold values from -8 to 8
- base_value_weight: bfloat16 [4096, 1024], P(('groups', 'seq')), parts along dimension 0, may hold values from -6 to 6
- shrink_a: bfloat16 [32, 8192, 192], P('groups', 'seq'), parts along dimension 0, may hold values from -0.0625 to 0.0625
- expand_q: bfloat16 [32, 64, 8192], P('groups', None, 'seq'), parts along dimension 0, may hold values from -0.375 to 0.375
- key_value_up_weight: bfloat16 [32, 64, 2048], P('groups'), parts along dimension 0, may hold values from -0.375 to 0.375
- block_request: int32 [64], P('groups'), parts along dimension 0, may hold values from 0 to 7, never falling along the last dimension, each value on 1 to 16 neighbouring positions
- request_adapter: int32 [16], P('groups'), parts along dimension 0, may hold values from 0 to 15
Outputs:
- attended: bfloat16 [4096, 8192], P(('groups', 'seq')), parts along dimension 0
There are 2 independent parts, one for each index of `groups`. A program takes and returns all parts, laid end to end along the dimension named above; each array names one. Nothing has to cross between parts.
Inputs may be any that keep to these rules, and one draw needn't show every extreme that they name: `block_request`: each request holds 1 to 16 consecutive blocks, request numbers never fall along the blocks, and some request holds exactly 16 blocks.
All inputs are finite; a program needn't handle non-finite values.
Results may differ from a plain program's by a relative error of at most 0.012.
The roundings to bfloat16 on the way count: a program that leaves them out, or rounds other values in their place, can miss the bound.
Values may be sent and summed in bfloat16 or wider, within the bound.
No kernel may reach another device: no remote copies, remote signals or barrier semaphores. Data moves between devices by JAX's collectives and lax.ppermute only.
A program may use at most 128 MiB of HBM per device.

v0:
```python
import math
import jax
import jax.numpy as jnp
from jax import lax
from jax.sharding import PartitionSpec as P

QUERY_HEADS = 64
KEY_VALUE_HEADS = 8
HEAD_SIZE = 128
ADAPTER_RANK = 64
QBLK = 512


def body(
    hidden,
    q_base,
    base_key_weight,
    base_value_weight,
    shrink_a,
    expand_q,
    key_value_up_weight,
    block_request,
    request_adapter,
):
    token_per_device = hidden.shape[0]
    device_list = lax.axis_size("seq")
    my_index = lax.axis_index("seq")
    token_total = token_per_device * device_list
    block_count = block_request.shape[0]
    block_len = token_total // block_count
    most_blocks = min(32, block_count // 2)
    key_window = QBLK + most_blocks * block_len
    heads_dev = QUERY_HEADS // device_list
    device_groups = device_list // KEY_VALUE_HEADS
    key_value_head = my_index // device_groups
    request_count = request_adapter.shape[0]
    adapter_number = key_value_up_weight.shape[0]
    slice_width = shrink_a.shape[1]
    picked = block_request[:, None] == jnp.arange(request_count, dtype=jnp.int32)[None, :]
    adapter_of = jnp.sum(jnp.where(picked, request_adapter[None, :], 0), axis=1)
    feature_rows = lax.all_to_all(hidden, "seq", split_axis=1, concat_axis=0, tiled=True)
    partial_value = jnp.einsum(
        "btf,bfr->btr",
        feature_rows.reshape(block_count, block_len, slice_width),
        shrink_a[adapter_of],
        preferred_element_type=jnp.float32,
    ).reshape(token_total, 3 * ADAPTER_RANK)
    shrunk = lax.psum(partial_value, "seq").astype(jnp.bfloat16)
    key_replicas = jnp.repeat(
        base_key_weight.reshape(token_per_device, KEY_VALUE_HEADS, HEAD_SIZE), device_groups, axis=1
    ).reshape(token_per_device, device_list * HEAD_SIZE)
    value_replicas = jnp.repeat(
        base_value_weight.reshape(token_per_device, KEY_VALUE_HEADS, HEAD_SIZE),
        device_groups,
        axis=1,
    ).reshape(token_per_device, device_list * HEAD_SIZE)
    q_heads, k_one, v_one = (
        lax.all_to_all(q_base, "seq", split_axis=1, concat_axis=0, tiled=True),
        lax.all_to_all(key_replicas, "seq", split_axis=1, concat_axis=0, tiled=True),
        lax.all_to_all(value_replicas, "seq", split_axis=1, concat_axis=0, tiled=True),
    )
    low_blocks = shrunk.reshape(block_count, block_len, 3, ADAPTER_RANK)
    q_delta = jnp.einsum(
        "btr,brc->btc",
        low_blocks[:, :, 0],
        expand_q[adapter_of],
        preferred_element_type=jnp.float32,
    ).reshape(token_total, heads_dev * HEAD_SIZE)
    query_rows = (
        (q_heads.astype(jnp.float32) + q_delta)
        .astype(jnp.bfloat16)
        .reshape(token_total, heads_dev, HEAD_SIZE)
    )
    kv_table = lax.dynamic_index_in_dim(
        key_value_up_weight.reshape(adapter_number, ADAPTER_RANK, 2, KEY_VALUE_HEADS, HEAD_SIZE),
        key_value_head,
        axis=3,
        keepdims=False,
    )
    kv_delta = jnp.einsum(
        "btcr,brcd->btcd",
        low_blocks[:, :, 1:],
        kv_table[adapter_of],
        preferred_element_type=jnp.float32,
    ).reshape(token_total, 2, HEAD_SIZE)
    key_rows = (k_one.astype(jnp.float32) + kv_delta[:, 0]).astype(jnp.bfloat16)
    value_rows = (v_one.astype(jnp.float32) + kv_delta[:, 1]).astype(jnp.bfloat16)
    request_of = jnp.repeat(block_request, block_len)
    score_scale = 1.0 / math.sqrt(HEAD_SIZE)

    def attend(block_index):
        q_start = block_index * QBLK
        k_start = jnp.clip(q_start + QBLK - key_window, 0, token_total - key_window)
        q_rows = lax.dynamic_slice_in_dim(query_rows, q_start, QBLK, 0)
        k_rows = lax.dynamic_slice_in_dim(key_rows, k_start, key_window, 0)
        v_rows = lax.dynamic_slice_in_dim(value_rows, k_start, key_window, 0)
        q_request = lax.dynamic_slice_in_dim(request_of, q_start, QBLK, 0)
        k_request = lax.dynamic_slice_in_dim(request_of, k_start, key_window, 0)
        q_pos = q_start + jnp.arange(QBLK, dtype=jnp.int32)
        k_pos = k_start + jnp.arange(key_window, dtype=jnp.int32)
        allowed = (k_pos[None, :] <= q_pos[:, None]) & (k_request[None, :] == q_request[:, None])
        scores = (
            jnp.einsum("qhd,kd->hqk", q_rows, k_rows, preferred_element_type=jnp.float32)
            * score_scale
        )
        scores = jnp.where(allowed[None], scores, -1e30)
        row_max = jnp.max(scores, axis=-1, keepdims=True)
        weights = jnp.exp(scores - row_max)
        probs = (weights / jnp.sum(weights, axis=-1, keepdims=True)).astype(jnp.bfloat16)
        result = jnp.einsum("hqk,kd->qhd", probs, v_rows, preferred_element_type=jnp.float32)
        return result.astype(jnp.bfloat16).reshape(QBLK, heads_dev * HEAD_SIZE)

    blocks_out = lax.map(attend, jnp.arange(token_total // QBLK, dtype=jnp.int32))
    head_rows = blocks_out.reshape(token_total, heads_dev * HEAD_SIZE)
    return lax.all_to_all(head_rows, "seq", split_axis=0, concat_axis=1, tiled=True)


def solution(mesh):
    return jax.shard_map(
        body,
        mesh=mesh,
        in_specs=(
            P(("groups", "seq"), None),
            P(("groups", "seq"), None),
            P(("groups", "seq"), None),
            P(("groups", "seq"), None),
            P("groups", "seq", None),
            P("groups", None, "seq"),
            P("groups", None, None),
            P("groups"),
            P("groups"),
        ),
        out_specs=P(("groups", "seq"), None),
        check_vma=False,
    )
```

profile of v0, /device:TPU:1, one launch (start us, length us, event | category | flops | bytes accessed | tf_op | source)
XLA Modules:
  0.0 373.0 jit_solution(3717521788086597597)
XLA Ops:
  0.0 1.1 copy_bitcast_fusion.3
  2.0 7.3 %all-to-all-start = ((bf16[128,16,128]{2,0,1:T(8,128)(2,1)}), bf16[128,16,128]{2,0,1:T(8,128)(2,1)}, u32[]{:S(2)}, u32[]{:S(2)}) async-start(bf16[128,16,128]{2,0,1:T(8,128)(2,1)} %bitcast.117), calls=%async_computation | async-start | bytes 1048576 | tf_op jit(solution)/shard_map/all_to_all | solution.py:60
  9.4 3.1 copy.96
  12.5 11.0 %all-to-all-done = bf16[128,16,128]{2,0,1:T(8,128)(2,1)} async-done(((bf16[128,16,128]{2,0,1:T(8,128)(2,1)}), bf16[128,16,128]{2,0,1:T(8,128)(2,1)}, u32[]{:S(2)}, u32[]{:S(2)}) %all-to-all-start) | async-done | bytes 524320 | tf_op jit(solution)/shard_map/all_to_all | solution.py:60
  23.5 4.5 %all-to-all-start.1 = ((bf16[128,16,512]{2,0,1:T(8,128)(2,1)}), bf16[128,16,512]{2,0,1:T(8,128)(2,1)}, u32[]{:S(2)}, u32[]{:S(2)}) async-start(bf16[128,16,512]{2,0,1:T(8,128)(2,1)} %bitcast.109), calls=%async_computation.1 | async-start | bytes 4194304 | tf_op jit(solution)/shard_map/all_to_all | solution.py:41
  28.0 4.1 %copy.70 = bf16[128,8192]{0,1:T(8,128)(2,1)} copy(bf16[128,8192]{1,0:T(8,128)(2,1)} %param.12) | data formatting | bytes 4194304 | tf_op args[1]
  32.1 37.6 %all-to-all-done.1 = bf16[128,16,512]{2,0,1:T(8,128)(2,1)} async-done(((bf16[128,16,512]{2,0,1:T(8,128)(2,1)}), bf16[128,16,512]{2,0,1:T(8,128)(2,1)}, u32[]{:S(2)}, u32[]{:S(2)}) %all-to-all-start.1) | async-done | bytes 2097184 | tf_op jit(solution)/shard_map/all_to_all | solution.py:41
  69.7 10.7 %all-to-all-start.3 = ((bf16[128,16,512]{0,2,1:T(8,128)(2,1)}), bf16[128,16,512]{0,2,1:T(8,128)(2,1)}, u32[]{:S(2)}, u32[]{:S(2)}) async-start(bf16[128,16,512]{0,2,1:T(8,128)(2,1)} %bitcast.107), calls=%async_computation.3 | async-start | bytes 4194304 | tf_op jit(solution)/shard_map/all_to_all | solution.py:58
  80.4 5.6 %copy.89 = bf16[128,8,16,128]{3,2,1,0:T(8,128)(2,1)} copy(bf16[128,8,16,128]{3,1,2,0:T(8,128)(2,1)} %bitcast.114) | data formatting | bytes 8388608
  86.0 3.5 constant_dynamic-slice_fusion
  89.4 1.0 copy.97
  90.5 2.7 gather_fusion
  93.2 3.6 gather_fusion.1
  96.8 3.3 gather_fusion.2
  101.0 5.5 %fusion.26 = f32[32,192,64]{1,2,0:T(8,128)S(1)} fusion(bf16[32,512,192]{1,2,0:T(8,128)(2,1)} %gather_fusion.1, bf16[32,64,512]{2,1,0:T(8,128)(2,1)} %bitcast.13), kind=kOutput, calls=%fused_computation.50 | convolution fusion | flops 402653184 | bytes 9961472 | tf_op jit(solution)/shard_map/btf,bfr->btr/dot_general | solution.py:42
  106.5 1.7 copy.66
  108.2 70.1 %all-reduce.1 = bf16[2048,192]{0,1:T(8,128)(2,1)S(1)} all-reduce(f32[2048,192]{0,1:T(8,128)} %copy.66), channel_id=1, replica_groups=mesh['groups'=2,'seq'=16] {'seq'}, use_global_device_ids=true, to_apply=%region_1.2 | all-reduce | flops 393216 | bytes 2359296 | tf_op jit(solution)/shard_map/psum | solution.py:48
  178.4 1.6 reshape.146
  180.1 1.1 copy-done.2
  183.6 4.2 %fusion.22 = f32[32,64,512]{2,1,0:T(8,128)} fusion(bf16[32,64,512]{2,1,0:T(8,128)(2,1)} %gather_fusion.2, bf16[32,64,1,64]{3,1,0,2:T(8,128)(2,1)S(1)} %copy.85), kind=kOutput, calls=%fused_computation.38 | convolution fusion | flops 134217728 | bytes 6553600 | tf_op jit(solution)/shard_map/btr,brc->btc/dot_general | solution.py:63
  187.8 5.3 %reshape.150 = f32[2048,4,128]{2,1,0:T(4,128)} reshape(f32[32,64,512]{2,1,0:T(8,128)} %fusion.22) | data formatting | bytes 8388608 | tf_op jit(solution)/shard_map/reshape | solution.py:68
  193.1 5.3 %copy.73 = f32[2048,4,128]{0,2,1:T(8,128)} copy(f32[2048,4,128]{2,1,0:T(4,128)} %reshape.150) | data formatting | bytes 8388608 | tf_op jit(solution)/shard_map/reshape | solution.py:68
  199.3 8.5 %all-to-all-start.2 = ((bf16[128,16,128]{2,0,1:T(8,128)(2,1)}), bf16[128,16,128]{2,0,1:T(8,128)(2,1)S(1)}, u32[]{:S(2)}, u32[]{:S(2)}) async-start(bf16[128,16,128]{2,0,1:T(8,128)(2,1)} %bitcast.19), calls=%async_computation.2 | async-start | bytes 1048576 | tf_op jit(solution)/shard_map/all_to_all | solution.py:59
  207.8 2.0 convert_bitcast_fusion
  209.8 4.4 %copy.71 = f32[16,128,512]{1,0,2:T(8,128)} copy(f32[16,128,512]{1,2,0:T(8,128)S(1)} %convert_bitcast_fusion) | data formatting | bytes 8388608 | tf_op jit(solution)/shard_map/convert_element_type | solution.py:70
  214.2 4.9 %reshape.153 = f32[2048,4,128]{0,2,1:T(8,128)} reshape(f32[16,128,512]{1,0,2:T(8,128)} %copy.71) | data formatting | bytes 8388608 | tf_op jit(solution)/shard_map/convert_element_type | solution.py:70
  219.1 5.4 %add_convert_fusion = bf16[2048,4,128]{0,2,1:T(8,128)(2,1)} fusion(f32[2048,4,128]{0,2,1:T(8,128)} %reshape.153, f32[2048,4,128]{0,2,1:T(8,128)} %copy.73), kind=kLoop, calls=%fused_computation.28 | loop fusion | flops 2097152 | bytes 10485760 | tf_op jit(solution)/shard_map/convert_element_type | solution.py:71
  224.5 2.0 fusion.18
  226.6 84.4 %while.14 = (s32[]{:T(128)}, bf16[4,512,512]{2,1,0:T(8,128)(2,1)}, s32[4]{0:T(128)S(1)}, bf16[2048,128]{1,0:T(8,128)(2,1)}, s32[2048]{0:T(1024)S(1)}, /*index=5*...) while((s32[]{:T(128)}, bf16[4,512,512]{2,1,0:T(8,128)(2,1)}, ...), condition=%wide.region_5.6_spmd, body=%wide.region_2.5_spmd.sunk | while | flops 1638403584 | bytes 57991952 | solution.py:113
  228.1 1.2 compare_and_fusion.2
  229.3 2.8 fusion.42
  232.1 8.9 %fusion.43 = (f32[4,512]{1,0:T(4,128)S(1)}, f32[4,512,1536]{1,2,0:T(8,128)}) fusion(f32[1536,512,4]{1,0,2:T(8,128)S(1)} %fusion.42, pred[512,1536]{0,1:T(8,128)(4,1)S(1)} %compare_and_fusion.2), kind=kOutput, calls=%fused_computation.49.clone.1 | output fusion | flops 18875904 | bytes 25960448 | tf_op jit(solution)/shard_map/while/body/eval_jaxpr/sub | solution.py:108
  241.0 5.6 %fusion.44 = bf16[128,4,512]{2,0,1:T(8,128)(2,1)S(1)} fusion(f32[4,512,1536]{1,2,0:T(8,128)} %get-tuple-element.245, f32[4,512]{1,0:T(4,128)S(1)} %get-tuple-element.246, bf16[2048,128]{1,0:T(8,128)(2,1)S(1)} %copy-done.5, s32[]{:T(128)S(6)} %min.11), kind=kOutput, calls=%fused_computation.13.clone.1 | convolution fusion | flops 811859968 | bytes 13508612 | tf_op jit(solution)/shard_map/while/body/eval_jaxpr/hqk,kd->qhd/dot_general | solution.py:110
  249.2 1.2 compare_and_fusion.2
  250.4 2.8 fusion.42
  253.2 8.9 %fusion.43 = (f32[4,512]{1,0:T(4,128)S(1)}, f32[4,512,1536]{1,2,0:T(8,128)}) fusion(f32[1536,512,4]{1,0,2:T(8,128)S(1)} %fusion.42, pred[512,1536]{0,1:T(8,128)(4,1)S(1)} %compare_and_fusion.2), kind=kOutput, calls=%fused_computation.49.clone.1 | output fusion | flops 18875904 | bytes 25960448 | tf_op jit(solution)/shard_map/while/body/eval_jaxpr/sub | solution.py:108
  262.1 5.6 %fusion.44 = bf16[128,4,512]{2,0,1:T(8,128)(2,1)S(1)} fusion(f32[4,512,1536]{1,2,0:T(8,128)} %get-tuple-element.245, f32[4,512]{1,0:T(4,128)S(1)} %get-tuple-element.246, bf16[2048,128]{1,0:T(8,128)(2,1)S(1)} %copy-done.5, s32[]{:T(128)S(6)} %min.11), kind=kOutput, calls=%fused_computation.13.clone.1 | convolution fusion | flops 811859968 | bytes 13508612 | tf_op jit(solution)/shard_map/while/body/eval_jaxpr/hqk,kd->qhd/dot_general | solution.py:110
  270.3 1.2 compare_and_fusion.2
  271.4 2.8 fusion.42
  274.3 8.9 %fusion.43 = (f32[4,512]{1,0:T(4,128)S(1)}, f32[4,512,1536]{1,2,0:T(8,128)}) fusion(f32[1536,512,4]{1,0,2:T(8,128)S(1)} %fusion.42, pred[512,1536]{0,1:T(8,128)(4,1)S(1)} %compare_and_fusion.2), kind=kOutput, calls=%fused_computation.49.clone.1 | output fusion | flops 18875904 | bytes 25960448 | tf_op jit(solution)/shard_map/while/body/eval_jaxpr/sub | solution.py:108
  283.2 5.6 %fusion.44 = bf16[128,4,512]{2,0,1:T(8,128)(2,1)S(1)} fusion(f32[4,512,1536]{1,2,0:T(8,128)} %get-tuple-element.245, f32[4,512]{1,0:T(4,128)S(1)} %get-tuple-element.246, bf16[2048,128]{1,0:T(8,128)(2,1)S(1)} %copy-done.5, s32[]{:T(128)S(6)} %min.11), kind=kOutput, calls=%fused_computation.13.clone.1 | convolution fusion | flops 811859968 | bytes 13508612 | tf_op jit(solution)/shard_map/while/body/eval_jaxpr/hqk,kd->qhd/dot_general | solution.py:110
  291.4 1.2 compare_and_fusion.2
  292.5 2.8 fusion.42
  295.4 8.9 %fusion.43 = (f32[4,512]{1,0:T(4,128)S(1)}, f32[4,512,1536]{1,2,0:T(8,128)}) fusion(f32[1536,512,4]{1,0,2:T(8,128)S(1)} %fusion.42, pred[512,1536]{0,1:T(8,128)(4,1)S(1)} %compare_and_fusion.2), kind=kOutput, calls=%fused_computation.49.clone.1 | output fusion | flops 18875904 | bytes 25960448 | tf_op jit(solution)/shard_map/while/body/eval_jaxpr/sub | solution.py:108
  304.3 5.6 %fusion.44 = bf16[128,4,512]{2,0,1:T(8,128)(2,1)S(1)} fusion(f32[4,512,1536]{1,2,0:T(8,128)} %get-tuple-element.245, f32[4,512]{1,0:T(4,128)S(1)} %get-tuple-element.246, bf16[2048,128]{1,0:T(8,128)(2,1)S(1)} %copy-done.5, s32[]{:T(128)S(6)} %min.11), kind=kOutput, calls=%fused_computation.13.clone.1 | convolution fusion | flops 811859968 | bytes 13508612 | tf_op jit(solution)/shard_map/while/body/eval_jaxpr/hqk,kd->qhd/dot_general | solution.py:110
  310.9 53.9 %all_to_all.74 = bf16[16,128,512]{2,1,0:T(8,128)(2,1)} all-to-all(bf16[16,128,512]{2,1,0:T(8,128)(2,1)} %bitcast.116), channel_id=1, replica_groups=mesh['groups'=2,'seq'=16] {'seq'}, dimensions={0} | all-to-all | bytes 4194304 | tf_op jit(solution)/shard_map/all_to_all | solution.py:115
  364.8 4.0 %copy.77 = bf16[128,16,512]{0,2,1:T(8,128)(2,1)} copy(bf16[128,16,512]{2,0,1:T(8,128)(2,1)} %bitcast.110) | data formatting | bytes 4194304 | tf_op jit(solution)/shard_map/all_to_all | solution.py:115
  368.9 4.1 %copy.78 = bf16[128,8192]{1,0:T(8,128)(2,1)} copy(bf16[128,8192]{0,1:T(8,128)(2,1)} %bitcast.111) | data formatting | bytes 4194304 | tf_op jit(solution)/shard_map/all_to_all | solution.py:115
  (69 shorter events, 12.7 us)
Async XLA Ops:
  0.0 93.2 %copy-start = (bf16[16,512,192]{1,2,0:T(8,128)(2,1)S(1)}, bf16[16,512,192]{1,2,0:T(8,128)(2,1)}, u32[]{:S(2)}) copy-start(bf16[16,512,192]{1,2,0:T(8,128)(2,1)} %param.15) | copy-start | bytes 9437188
  2.0 21.4 %all-to-all-start = ((bf16[128,16,128]{2,0,1:T(8,128)(2,1)}), bf16[128,16,128]{2,0,1:T(8,128)(2,1)}, u32[]{:S(2)}, u32[]{:S(2)}) async-start(bf16[128,16,128]{2,0,1:T(8,128)(2,1)} %bitcast.117), calls=%async_computation | async-start | bytes 1048576 | tf_op jit(solution)/shard_map/all_to_all | solution.py:60
  23.5 46.2 %all-to-all-start.1 = ((bf16[128,16,512]{2,0,1:T(8,128)(2,1)}), bf16[128,16,512]{2,0,1:T(8,128)(2,1)}, u32[]{:S(2)}, u32[]{:S(2)}) async-start(bf16[128,16,512]{2,0,1:T(8,128)(2,1)} %bitcast.109), calls=%async_computation.1 | async-start | bytes 4194304 | tf_op jit(solution)/shard_map/all_to_all | solution.py:41
  69.7 128.7 %all-to-all-start.3 = ((bf16[128,16,512]{0,2,1:T(8,128)(2,1)}), bf16[128,16,512]{0,2,1:T(8,128)(2,1)}, u32[]{:S(2)}, u32[]{:S(2)}) async-start(bf16[128,16,512]{0,2,1:T(8,128)(2,1)} %bitcast.107), calls=%async_computation.3 | async-start | bytes 4194304 | tf_op jit(solution)/shard_map/all_to_all | solution.py:58
  85.9 4.4 %copy-start.7 = (s32[32]{0:T(128)S(1)}, s32[32]{0:T(128)}, u32[]{:S(2)}) copy-start(s32[32]{0:T(128)} %param.18) | copy-start | bytes 388
  86.0 4.4 %copy-start.8 = (s32[8]{0:T(128)S(1)}, s32[8]{0:T(128)}, u32[]{:S(2)}) copy-start(s32[8]{0:T(128)} %param.19) | copy-start | bytes 100
  96.8 3.4 copy-start.6
  178.4 2.8 copy-start.3
  180.0 1.2 copy-start.2
  181.9 1.0 slice-start
  193.1 5.4 %copy-start.4 = (bf16[128,8,128]{2,0,1:T(8,128)(2,1)S(1)}, bf16[128,8,128]{2,0,1:T(8,128)(2,1)}, u32[]{:S(2)}) copy-start(bf16[128,8,128]{2,0,1:T(8,128)(2,1)} %copy_bitcast_fusion.2) | copy-start | bytes 786436
  199.3 25.2 %all-to-all-start.2 = ((bf16[128,16,128]{2,0,1:T(8,128)(2,1)}), bf16[128,16,128]{2,0,1:T(8,128)(2,1)S(1)}, u32[]{:S(2)}, u32[]{:S(2)}) async-start(bf16[128,16,128]{2,0,1:T(8,128)(2,1)} %bitcast.19), calls=%async_computation.2 | async-start | bytes 1048576 | tf_op jit(solution)/shard_map/all_to_all | solution.py:59
  232.1 8.9 %copy-start.5 = (bf16[2048,128]{1,0:T(8,128)(2,1)S(1)}, bf16[2048,128]{1,0:T(8,128)(2,1)}, u32[]{:S(2)}) copy-start(bf16[2048,128]{1,0:T(8,128)(2,1)} %get-tuple-element.276) | copy-start | bytes 1572868 | tf_op jit(solution)/shard_map/while
  253.2 8.9 %copy-start.5 = (bf16[2048,128]{1,0:T(8,128)(2,1)S(1)}, bf16[2048,128]{1,0:T(8,128)(2,1)}, u32[]{:S(2)}) copy-start(bf16[2048,128]{1,0:T(8,128)(2,1)} %get-tuple-element.276) | copy-start | bytes 1572868 | tf_op jit(solution)/shard_map/while
  274.3 8.9 %copy-start.5 = (bf16[2048,128]{1,0:T(8,128)(2,1)S(1)}, bf16[2048,128]{1,0:T(8,128)(2,1)}, u32[]{:S(2)}) copy-start(bf16[2048,128]{1,0:T(8,128)(2,1)} %get-tuple-element.276) | copy-start | bytes 1572868 | tf_op jit(solution)/shard_map/while
  295.4 8.9 %copy-start.5 = (bf16[2048,128]{1,0:T(8,128)(2,1)S(1)}, bf16[2048,128]{1,0:T(8,128)(2,1)}, u32[]{:S(2)}) copy-start(bf16[2048,128]{1,0:T(8,128)(2,1)} %get-tuple-element.276) | copy-start | bytes 1572868 | tf_op jit(solution)/shard_map/while
  364.8 8.1 %copy-start.1 = (bf16[16,512,192]{1,2,0:T(8,128)(2,1)S(1)}, bf16[16,512,192]{1,2,0:T(8,128)(2,1)}, u32[]{:S(2)}) copy-start(bf16[16,512,192]{1,2,0:T(8,128)(2,1)} %param.15) | copy-start | bytes 9437188
where the time goes:
time: 375 us; the launch traced here: 373 us
  blocking collectives  124 us (33%)
  local copies, waits for them, and re-layouts  72.3 us (19%)
  other arithmetic  49.8 us (13%)
  waiting for transfers between devices  48.6 us (13%)
  matrix products  44.2 us (12%)
  starting transfers between devices  31 us (8%)
    psum x1, blocking collectives, body(): shrunk = lax.psum(partial_value, 'seq').astype(jnp.bfloat16)  70.1 us
    all_to_all x1, blocking collectives, body(): lax.all_to_all(head_rows, 'seq', split_axis=0, concat_axis=1, tiled=True)  53.9 us
    all_to_all x1, waiting for transfers between devices, body(): lax.all_to_all(hidden, 'seq', split_axis=1, concat_axis=0, tiled=True)  37.6 us
    sub x4, other arithmetic, attend(): weights = jnp.exp(scores - row_max)  35.6 us
    dot_general x4, matrix products, attend(): jnp.einsum('hqk,kd->qhd', probs, v_rows, preferred_element_type=jnp.float32)  22.5 us
    unnamed x19, local copies, waits for them, and re-layouts  11.3 us
    dot_general x4, matrix products, attend(): jnp.einsum('qhd,kd->hqk', q_rows, k_rows, preferred_element_type=jnp.floa...  11.3 us
    all_to_all x1, waiting for transfers between devices, body(): lax.all_to_all(value_replicas, 'seq', split_axis=1, concat_axis=0, tiled=...  11 us
  transfers between devices with their start and end apart: 4, of which 2 were waited for; matrix products, arithmetic and copies ran while one was open for 19% of the time, Pallas kernels for 0%

commit v1 on v0

--- a/solution.py
+++ b/solution.py
@@ -45,7 +45,7 @@
         shrink_a[adapter_of],
         preferred_element_type=jnp.float32,
     ).reshape(token_total, 3 * ADAPTER_RANK)
-    shrunk = lax.psum(partial_value, "seq").astype(jnp.bfloat16)
+    shrunk = jnp.sum(lax.all_gather(partial_value, "seq"), axis=0).astype(jnp.bfloat16)
     key_replicas = jnp.repeat(
         base_key_weight.reshape(token_per_device, KEY_VALUE_HEADS, HEAD_SIZE), device_groups, axis=1
     ).reshape(token_per_device, device_list * HEAD_SIZE)

time: 375 us -> 454 us (1.21)
  waiting for transfers between devices: 48.6 us -> 171 us
  blocking collectives: 124 us -> 53.8 us
  between operations: 0.13 us -> 13.5 us
  other arithmetic: 49.8 us -> 57.5 us
  starting transfers between devices: 31 us -> 37.2 us
    psum x1 -> x0, blocking collectives: 70.1 us -> none  [body(): shrunk = lax.psum(partial_value, 'seq').astype(jnp.bfloat16)]
    all_to_all x1, waiting for transfers between devices: 0.01 us -> 67.2 us  [body(): lax.all_to_all(q_base, 'seq', split_axis=1, concat_axis=0, tiled=True)]
    all_gather x0 -> x1, waiting for transfers between devices: none -> 65.6 us  [body(): lax.all_gather(partial_value, 'seq')]
    all_to_all x1, waiting for transfers between devices: 11 us -> 0.01 us  [body(): lax.all_to_all(value_replicas, 'seq', split_axis=1, concat_axis=0, tiled=...]
    reduce_sum x0 -> x1, other arithmetic: none -> 9.19 us  [body(): jnp.sum(lax.all_gather(partial_value, 'seq'), axis=0).astype(jnp.bfloat16)]
    all_to_all x1, starting transfers between devices: 8.48 us -> 14.2 us  [body(): lax.all_to_all(key_replicas, 'seq', split_axis=1, concat_axis=0, tiled=True)]
    unnamed x19 -> x25, local copies, waits for them, and re-layouts: 11.3 us -> 12.2 us
  transfers between devices with their start and end apart: 4 -> 5, of which waited for: 2 -> 3; matrix products, arithmetic and copies ran while one was open for 19% -> 16% of each run, Pallas kernels for 0% -> 0%
where the time goes in v1:
time: 454 us; the launch traced here: 452 us
  waiting for transfers between devices  171 us (38%)
  local copies, waits for them, and re-layouts  73 us (16%)
  other arithmetic  57.5 us (13%)
  blocking collectives  53.8 us (12%)
  matrix products  43.7 us (10%)
  starting transfers between devices  37.2 us (8%)
  between operations  13.5 us (3%)
    all_to_all x1, waiting for transfers between devices, body(): lax.all_to_all(q_base, 'seq', split_axis=1, concat_axis=0, tiled=True)  67.2 us
    all_gather x1, waiting for transfers between devices, body(): lax.all_gather(partial_value, 'seq')  65.6 us
    all_to_all x1, blocking collectives, body(): lax.all_to_all(head_rows, 'seq', split_axis=0, concat_axis=1, tiled=True)  53.8 us
    all_to_all x1, waiting for transfers between devices, body(): lax.all_to_all(hidden, 'seq', split_axis=1, concat_axis=0, tiled=True)  37.8 us
    sub x4, other arithmetic, attend(): weights = jnp.exp(scores - row_max)  35.5 us
    dot_general x4, matrix products, attend(): jnp.einsum('hqk,kd->qhd', probs, v_rows, preferred_element_type=jnp.float32)  22.5 us
    all_to_all x1, starting transfers between devices, body(): lax.all_to_all(key_replicas, 'seq', split_axis=1, concat_axis=0, tiled=True)  14.2 us
    unnamed x25, local copies, waits for them, and re-layouts  12.2 us
  transfers between devices with their start and end apart: 5, of which 3 were waited for; matrix products, arithmetic and copies ran while one was open for 16% of the time, Pallas kernels for 0%

profile of v1, /device:TPU:1, one launch (start us, length us, event | category | flops | bytes accessed | tf_op | source)
XLA Modules:
  0.0 452.1 jit_solution(3502599225387007100)
XLA Ops:
  6.5 3.3 copy.118
  9.8 7.5 %all-to-all-start.1 = ((bf16[128,16,512]{2,0,1:T(8,128)(2,1)}), bf16[128,16,512]{2,0,1:T(8,128)(2,1)}, u32[]{:S(2)}, u32[]{:S(2)}) async-start(bf16[128,16,512]{2,0,1:T(8,128)(2,1)} %bitcast.109), calls=%async_computation.1 | async-start | bytes 4194304 | tf_op jit(solution)/shard_map/all_to_all | solution.py:41
  17.5 3.6 gather_fusion.1
  21.1 37.8 %all-to-all-done.1 = bf16[128,16,512]{2,0,1:T(8,128)(2,1)} async-done(((bf16[128,16,512]{2,0,1:T(8,128)(2,1)}), bf16[128,16,512]{2,0,1:T(8,128)(2,1)}, u32[]{:S(2)}, u32[]{:S(2)}) %all-to-all-start.1) | async-done | bytes 2097184 | tf_op jit(solution)/shard_map/all_to_all | solution.py:41
  58.9 5.5 %fusion.26 = f32[32,192,64]{1,2,0:T(8,128)S(1)} fusion(bf16[32,512,192]{1,2,0:T(8,128)(2,1)} %gather_fusion.1, bf16[32,64,512]{2,1,0:T(8,128)(2,1)} %bitcast.13), kind=kOutput, calls=%fused_computation.50 | convolution fusion | flops 402653184 | bytes 9961472 | tf_op jit(solution)/shard_map/btf,bfr->btr/dot_general | solution.py:42
  64.5 1.8 copy.85
  66.2 4.1 copy.91
  70.3 10.7 %all-to-all-start.3 = ((bf16[128,16,512]{0,2,1:T(8,128)(2,1)}), bf16[128,16,512]{0,2,1:T(8,128)(2,1)S(1)}, u32[]{:S(2)}, u32[]{:S(2)}) async-start(bf16[128,16,512]{0,2,1:T(8,128)(2,1)} %bitcast.107), calls=%async_computation.3 | async-start | bytes 4194304 | tf_op jit(solution)/shard_map/all_to_all | solution.py:58
  81.0 5.6 %copy.111 = bf16[128,8,16,128]{3,2,1,0:T(8,128)(2,1)} copy(bf16[128,8,16,128]{3,1,2,0:T(8,128)(2,1)} %bitcast.114) | data formatting | bytes 8388608
  86.7 67.2 %all-to-all-done.3 = bf16[128,16,512]{0,2,1:T(8,128)(2,1)S(1)} async-done(((bf16[128,16,512]{0,2,1:T(8,128)(2,1)}), bf16[128,16,512]{0,2,1:T(8,128)(2,1)S(1)}, u32[]{:S(2)}, u32[]{:S(2)}) %all-to-all-start.3) | async-done | bytes 2097184 | tf_op jit(solution)/shard_map/all_to_all | solution.py:58
  154.8 4.8 %all-to-all-start = ((bf16[128,16,128]{2,0,1:T(8,128)(2,1)}), bf16[128,16,128]{2,0,1:T(8,128)(2,1)}, u32[]{:S(2)}, u32[]{:S(2)}) async-start(bf16[128,16,128]{2,0,1:T(8,128)(2,1)} %bitcast.6), calls=%async_computation | async-start | bytes 1048576 | tf_op jit(solution)/shard_map/all_to_all | solution.py:60
  159.6 4.6 %constant_dynamic-slice_fusion = bf16[16,64,2,1,128]{4,3,2,1,0:T(2,128)(2,1)} fusion(bf16[16,64,2,8,128]{4,3,2,1,0:T(8,128)(2,1)} %bitcast.112, s32[]{:T(128)S(6)} %select_n.49), kind=kLoop, calls=%fused_computation.48 | loop fusion | bytes 1048580 | tf_op jit(solution)/shard_map/jit(dynamic_index_in_dim)/dynamic_slice | solution.py:74
  164.2 1.4 copy.119
  165.6 1.7 gather_fusion
  167.2 3.2 gather_fusion.2
  171.8 4.4 copy.92
  176.2 5.0 %reshape.148 = f32[2048,4,128]{0,2,1:T(8,128)} reshape(f32[16,128,512]{1,0,2:T(8,128)} %copy.92) | data formatting | bytes 8388608 | tf_op jit(solution)/shard_map/convert_element_type | solution.py:70
  181.1 65.6 %all-gather.2.cloned.1.call-done = f32[16,2048,192]{1,2,0:T(8,128)} async-done(((f32[1,2048,192]{1,2,0:T(8,128)}), f32[16,2048,192]{1,2,0:T(8,128)}) %all-gather.2.cloned.1.call-update) | async-done | bytes 25165840 | tf_op jit(solution)/shard_map/all_gather | solution.py:48
  246.7 9.2 %reduce_sum.37 = bf16[2048,192]{0,1:T(8,128)(2,1)S(1)} reduce(f32[16,2048,192]{1,2,0:T(8,128)} %all-gather.2.cloned.1.call-done, f32[]{:T(128)} %constant.110.clone.1), dimensions={0}, to_apply=%region_1.2 | reduce | flops 5898240 | bytes 25952260 | tf_op jit(solution)/shard_map/reduce_sum | solution.py:48
  255.9 1.6 convert_element_type.70
  259.5 1.5 copy.89
  261.0 1.4 copy.107
  263.3 14.2 %all-to-all-start.2 = ((bf16[128,16,128]{2,0,1:T(8,128)(2,1)}), bf16[128,16,128]{2,0,1:T(8,128)(2,1)S(1)}, u32[]{:S(2)}, u32[]{:S(2)}) async-start(bf16[128,16,128]{2,0,1:T(8,128)(2,1)} %bitcast.19), calls=%async_computation.2 | async-start | bytes 1048576 | tf_op jit(solution)/shard_map/all_to_all | solution.py:59
  277.5 3.7 fusion.22
  281.2 5.3 %reshape.145 = f32[2048,4,128]{2,1,0:T(4,128)} reshape(f32[32,64,512]{2,1,0:T(8,128)} %fusion.22) | data formatting | bytes 8388608 | tf_op jit(solution)/shard_map/reshape | solution.py:68
  286.5 5.3 %copy.94 = f32[2048,4,128]{0,2,1:T(8,128)} copy(f32[2048,4,128]{2,1,0:T(4,128)} %reshape.145) | data formatting | bytes 8388608 | tf_op jit(solution)/shard_map/reshape | solution.py:68
  291.8 5.6 %add_convert_fusion = bf16[2048,4,128]{0,2,1:T(8,128)(2,1)} fusion(f32[2048,4,128]{0,2,1:T(8,128)} %reshape.148, f32[2048,4,128]{0,2,1:T(8,128)} %copy.94), kind=kLoop, calls=%fused_computation.28 | loop fusion | flops 2097152 | bytes 10485760 | tf_op jit(solution)/shard_map/convert_element_type | solution.py:71
  297.4 2.0 fusion.18
  299.4 83.9 %while.14 = (s32[]{:T(128)}, bf16[4,512,512]{2,1,0:T(8,128)(2,1)}, s32[4]{0:T(128)S(1)}, bf16[2048,128]{1,0:T(8,128)(2,1)}, s32[2048]{0:T(1024)S(1)}, /*index=5*...) while((s32[]{:T(128)}, bf16[4,512,512]{2,1,0:T(8,128)(2,1)}, ...), condition=%wide.region_5.6_spmd, body=%wide.region_2.5_spmd.sunk | while | flops 1638403584 | bytes 57991952 | solution.py:113
  300.8 1.2 compare_and_fusion.2
  302.0 2.8 fusion.42
  304.8 8.9 %fusion.43 = (f32[4,512]{1,0:T(4,128)S(1)}, f32[4,512,1536]{1,2,0:T(8,128)}) fusion(f32[1536,512,4]{1,0,2:T(8,128)S(1)} %fusion.42, pred[512,1536]{0,1:T(8,128)(4,1)S(1)} %compare_and_fusion.2), kind=kOutput, calls=%fused_computation.49.clone.1 | output fusion | flops 18875904 | bytes 25960448 | tf_op jit(solution)/shard_map/while/body/eval_jaxpr/sub | solution.py:108
  313.7 5.6 %fusion.44 = bf16[128,4,512]{2,0,1:T(8,128)(2,1)S(1)} fusion(f32[4,512,1536]{1,2,0:T(8,128)} %get-tuple-element.252, f32[4,512]{1,0:T(4,128)S(1)} %get-tuple-element.253, bf16[2048,128]{1,0:T(8,128)(2,1)S(1)} %copy-done.7, s32[]{:T(128)S(6)} %min.11), kind=kOutput, calls=%fused_computation.13.clone.1 | convolution fusion | flops 811859968 | bytes 13508612 | tf_op jit(solution)/shard_map/while/body/eval_jaxpr/hqk,kd->qhd/dot_general | solution.py:110
  321.8 1.2 compare_and_fusion.2
  323.0 2.8 fusion.42
  325.8 8.9 %fusion.43 = (f32[4,512]{1,0:T(4,128)S(1)}, f32[4,512,1536]{1,2,0:T(8,128)}) fusion(f32[1536,512,4]{1,0,2:T(8,128)S(1)} %fusion.42, pred[512,1536]{0,1:T(8,128)(4,1)S(1)} %compare_and_fusion.2), kind=kOutput, calls=%fused_computation.49.clone.1 | output fusion | flops 18875904 | bytes 25960448 | tf_op jit(solution)/shard_map/while/body/eval_jaxpr/sub | solution.py:108
  334.7 5.6 %fusion.44 = bf16[128,4,512]{2,0,1:T(8,128)(2,1)S(1)} fusion(f32[4,512,1536]{1,2,0:T(8,128)} %get-tuple-element.252, f32[4,512]{1,0:T(4,128)S(1)} %get-tuple-element.253, bf16[2048,128]{1,0:T(8,128)(2,1)S(1)} %copy-done.7, s32[]{:T(128)S(6)} %min.11), kind=kOutput, calls=%fused_computation.13.clone.1 | convolution fusion | flops 811859968 | bytes 13508612 | tf_op jit(solution)/shard_map/while/body/eval_jaxpr/hqk,kd->qhd/dot_general | solution.py:110
  342.8 1.2 compare_and_fusion.2
  343.9 2.8 fusion.42
  346.8 8.9 %fusion.43 = (f32[4,512]{1,0:T(4,128)S(1)}, f32[4,512,1536]{1,2,0:T(8,128)}) fusion(f32[1536,512,4]{1,0,2:T(8,128)S(1)} %fusion.42, pred[512,1536]{0,1:T(8,128)(4,1)S(1)} %compare_and_fusion.2), kind=kOutput, calls=%fused_computation.49.clone.1 | output fusion | flops 18875904 | bytes 25960448 | tf_op jit(solution)/shard_map/while/body/eval_jaxpr/sub | solution.py:108
  355.6 5.6 %fusion.44 = bf16[128,4,512]{2,0,1:T(8,128)(2,1)S(1)} fusion(f32[4,512,1536]{1,2,0:T(8,128)} %get-tuple-element.252, f32[4,512]{1,0:T(4,128)S(1)} %get-tuple-element.253, bf16[2048,128]{1,0:T(8,128)(2,1)S(1)} %copy-done.7, s32[]{:T(128)S(6)} %min.11), kind=kOutput, calls=%fused_computation.13.clone.1 | convolution fusion | flops 811859968 | bytes 13508612 | tf_op jit(solution)/shard_map/while/body/eval_jaxpr/hqk,kd->qhd/dot_general | solution.py:110
  363.7 1.2 compare_and_fusion.2
  364.9 2.8 fusion.42
  367.7 8.9 %fusion.43 = (f32[4,512]{1,0:T(4,128)S(1)}, f32[4,512,1536]{1,2,0:T(8,128)}) fusion(f32[1536,512,4]{1,0,2:T(8,128)S(1)} %fusion.42, pred[512,1536]{0,1:T(8,128)(4,1)S(1)} %compare_and_fusion.2), kind=kOutput, calls=%fused_computation.49.clone.1 | output fusion | flops 18875904 | bytes 25960448 | tf_op jit(solution)/shard_map/while/body/eval_jaxpr/sub | solution.py:108
  376.6 5.6 %fusion.44 = bf16[128,4,512]{2,0,1:T(8,128)(2,1)S(1)} fusion(f32[4,512,1536]{1,2,0:T(8,128)} %get-tuple-element.252, f32[4,512]{1,0:T(4,128)S(1)} %get-tuple-element.253, bf16[2048,128]{1,0:T(8,128)(2,1)S(1)} %copy-done.7, s32[]{:T(128)S(6)} %min.11), kind=kOutput, calls=%fused_computation.13.clone.1 | convolution fusion | flops 811859968 | bytes 13508612 | tf_op jit(solution)/shard_map/while/body/eval_jaxpr/hqk,kd->qhd/dot_general | solution.py:110
  383.3 53.8 %all_to_all.74 = bf16[16,128,512]{2,1,0:T(8,128)(2,1)} all-to-all(bf16[16,128,512]{2,1,0:T(8,128)(2,1)} %bitcast.116), channel_id=1, replica_groups=mesh['groups'=2,'seq'=16] {'seq'}, dimensions={0} | all-to-all | bytes 4194304 | tf_op jit(solution)/shard_map/all_to_all | solution.py:115
  437.1 4.1 copy.98
  441.2 4.1 copy.99
  (78 shorter events, 12.5 us)
Async XLA Ops:
  6.5 10.9 %copy-start = (bf16[16,512,192]{1,2,0:T(8,128)(2,1)S(1)}, bf16[16,512,192]{1,2,0:T(8,128)(2,1)}, u32[]{:S(2)}) copy-start(bf16[16,512,192]{1,2,0:T(8,128)(2,1)} %param.15) | copy-start | bytes 9437188
  9.8 7.5 %copy-start.10 = (s32[32]{0:T(128)S(1)}, s32[32]{0:T(128)}, u32[]{:S(2)}) copy-start(s32[32]{0:T(128)} %param.18) | copy-start | bytes 388
  9.8 7.5 %copy-start.11 = (s32[8]{0:T(128)S(1)}, s32[8]{0:T(128)}, u32[]{:S(2)}) copy-start(s32[8]{0:T(128)} %param.19) | copy-start | bytes 100
  9.8 49.1 %all-to-all-start.1 = ((bf16[128,16,512]{2,0,1:T(8,128)(2,1)}), bf16[128,16,512]{2,0,1:T(8,128)(2,1)}, u32[]{:S(2)}, u32[]{:S(2)}) async-start(bf16[128,16,512]{2,0,1:T(8,128)(2,1)} %bitcast.109), calls=%async_computation.1 | async-start | bytes 4194304 | tf_op jit(solution)/shard_map/all_to_all | solution.py:41
  17.3 229.4 %all-gather.2.cloned.1.call-start = ((), (), s32[]{:S(2)}) async-start(), calls=%async_computation.5 | async-start | bytes 26738688 | tf_op jit(solution)/shard_map/all_gather | solution.py:48
  70.3 83.6 %all-to-all-start.3 = ((bf16[128,16,512]{0,2,1:T(8,128)(2,1)}), bf16[128,16,512]{0,2,1:T(8,128)(2,1)S(1)}, u32[]{:S(2)}, u32[]{:S(2)}) async-start(bf16[128,16,512]{0,2,1:T(8,128)(2,1)} %bitcast.107), calls=%async_computation.3 | async-start | bytes 4194304 | tf_op jit(solution)/shard_map/all_to_all | solution.py:58
  81.0 5.6 %copy-start.8 = (bf16[128,1024]{1,0:T(8,128)(2,1)S(1)}, bf16[128,1024]{1,0:T(8,128)(2,1)}, u32[]{:S(2)}) copy-start(bf16[128,1024]{1,0:T(8,128)(2,1)} %param.14) | copy-start | bytes 786436
  154.8 107.7 %all-to-all-start = ((bf16[128,16,128]{2,0,1:T(8,128)(2,1)}), bf16[128,16,128]{2,0,1:T(8,128)(2,1)}, u32[]{:S(2)}, u32[]{:S(2)}) async-start(bf16[128,16,128]{2,0,1:T(8,128)(2,1)} %bitcast.6), calls=%async_computation | async-start | bytes 1048576 | tf_op jit(solution)/shard_map/all_to_all | solution.py:60
  165.6 5.0 %copy-start.9 = (bf16[128,1024]{1,0:T(8,128)(2,1)S(1)}, bf16[128,1024]{1,0:T(8,128)(2,1)}, u32[]{:S(2)}) copy-start(bf16[128,1024]{1,0:T(8,128)(2,1)} %param.13) | copy-start | bytes 786436
  255.9 2.9 copy-start.5
  257.6 1.2 copy-start.4
  259.5 1.5 slice-start
  259.5 2.9 copy-start.6
  259.5 18.0 %copy-start.2 = (bf16[32,64,512]{2,1,0:T(8,128)(2,1)S(1)}, bf16[32,64,512]{2,1,0:T(8,128)(2,1)}, u32[]{:S(2)}) copy-start(bf16[32,64,512]{2,1,0:T(8,128)(2,1)} %gather_fusion.2) | copy-start | bytes 6291460
  263.3 34.0 %all-to-all-start.2 = ((bf16[128,16,128]{2,0,1:T(8,128)(2,1)}), bf16[128,16,128]{2,0,1:T(8,128)(2,1)S(1)}, u32[]{:S(2)}, u32[]{:S(2)}) async-start(bf16[128,16,128]{2,0,1:T(8,128)(2,1)} %bitcast.19), calls=%async_computation.2 | async-start | bytes 1048576 | tf_op jit(solution)/shard_map/all_to_all | solution.py:59
  291.8 5.6 %copy-start.3 = (f32[32,64,2,128]{3,1,0,2:T(8,128)S(1)}, f32[32,64,2,128]{3,1,0,2:T(8,128)}, u32[]{:S(2)}) copy-start(f32[32,64,2,128]{3,1,0,2:T(8,128)} %copy.89) | copy-start | bytes 6291460
  304.8 8.9 %copy-start.7 = (bf16[2048,128]{1,0:T(8,128)(2,1)S(1)}, bf16[2048,128]{1,0:T(8,128)(2,1)}, u32[]{:S(2)}) copy-start(bf16[2048,128]{1,0:T(8,128)(2,1)} %get-tuple-element.283) | copy-start | bytes 1572868 | tf_op jit(solution)/shard_map/while
  325.8 8.9 %copy-start.7 = (bf16[2048,128]{1,0:T(8,128)(2,1)S(1)}, bf16[2048,128]{1,0:T(8,128)(2,1)}, u32[]{:S(2)}) copy-start(bf16[2048,128]{1,0:T(8,128)(2,1)} %get-tuple-element.283) | copy-start | bytes 1572868 | tf_op jit(solution)/shard_map/while
  346.7 8.9 %copy-start.7 = (bf16[2048,128]{1,0:T(8,128)(2,1)S(1)}, bf16[2048,128]{1,0:T(8,128)(2,1)}, u32[]{:S(2)}) copy-start(bf16[2048,128]{1,0:T(8,128)(2,1)} %get-tuple-element.283) | copy-start | bytes 1572868 | tf_op jit(solution)/shard_map/while
  367.7 8.9 %copy-start.7 = (bf16[2048,128]{1,0:T(8,128)(2,1)S(1)}, bf16[2048,128]{1,0:T(8,128)(2,1)}, u32[]{:S(2)}) copy-start(bf16[2048,128]{1,0:T(8,128)(2,1)} %get-tuple-element.283) | copy-start | bytes 1572868 | tf_op jit(solution)/shard_map/while
  437.1 8.1 %copy-start.1 = (bf16[16,512,192]{1,2,0:T(8,128)(2,1)S(1)}, bf16[16,512,192]{1,2,0:T(8,128)(2,1)}, u32[]{:S(2)}) copy-start(bf16[16,512,192]{1,2,0:T(8,128)(2,1)} %param.15) | copy-start | bytes 9437188
Sparse Core Ops, SparseCore 0:
  66.3 180.3 all-gather.1
